TPU v7x, 128 devices: a whole 4x4x4 slice. The times are simulated.
128 devices in a mesh: chord: 4 (over x_lo, core), normal: 32 (over x_hi, y, z).
Axes of the slice: x: 4 (x_hi: 2, x_lo: 2; x = x_hi * 2 + x_lo), y: 4, z: 4, core: 2. Of those that a mesh axis runs over, the one named last changes fastest.
Arguments:
- direct_modes: bfloat16 [16, 5, 64, 512, 256], P(None, None, 'chord', 'normal'), may hold values from -62 to 62
- adjoint_modes: bfloat16 [16, 5, 64, 512, 256], P(None, None, 'chord', 'normal'), may hold values from -5 to 5
- base_flow: float32 [5, 64, 512, 256], P(None, 'chord', 'normal'), may hold values from -5 to 5
- cell_type: int32 [64, 512, 256], P('chord', 'normal'), may hold values from 0 to 2
- mode_pick: int32 [16], replicated, may hold values from 0 to 15, each once
- flux_mix: float32 [3, 5, 5], replicated, may hold values from -2.5 to 2.5
Outputs:
- sensitivity: float32 [5, 64, 512, 256], P(None, 'chord', 'normal')
Inputs may be any that keep to these rules, and one draw needn't show every extreme that they name: `mode_pick`: each mode once.
All inputs are finite; a program needn't handle non-finite values.
Results may differ from a plain program's by a relative error of at most 0.0003.
Values may be sent and summed in bfloat16 or wider, within the bound.
A program may use at most 256 MiB of HBM per device.

v0:
```python
import jax
import jax.numpy as jnp
from jax import lax
from jax.sharding import PartitionSpec as P


def with_halo(cells, sides, width):
    for axis, dim in sides:
        count = lax.axis_size(axis)
        ends = count - 1
        head = lax.slice_in_dim(cells, 0, width, axis=dim)
        tail = lax.slice_in_dim(cells, cells.shape[dim] - width, cells.shape[dim], axis=dim)
        cells = jnp.concatenate(
            [
                lax.ppermute(tail, axis, [(i, (i + 1) % count) for i in range(ends)]),
                cells,
                lax.ppermute(head, axis, [((i + 1) % count, i) for i in range(ends)]),
            ],
            axis=dim,
        )
    return cells


def mixing(matrix, field_in):
    return jnp.einsum("ij,i...->j...", matrix, field_in, precision=lax.Precision.HIGHEST)


def diff_chord(padded):
    return padded[..., 2:, 1:-1, :] - padded[..., :-2, 1:-1, :]


def diff_normal(padded):
    return padded[..., 1:-1, 2:, :] - padded[..., 1:-1, :-2, :]


def inner_cells(padded):
    return padded[..., 1:-1, 1:-1, :]


def diff_span(field_in):
    return jnp.roll(field_in, -1, -1) - jnp.roll(field_in, 1, -1)


def bilinear_term(left_pad, right_pad, flux_mix):
    summed = jnp.zeros(inner_cells(left_pad).shape, jnp.float32)
    for axis_num, differ in ((0, diff_chord), (1, diff_normal)):
        mixed_adj = mixing(flux_mix[axis_num], right_pad)
        summed = summed + differ(left_pad) * inner_cells(mixed_adj) - differ(left_pad * mixed_adj)
    left_in = inner_cells(left_pad)
    mixed_adj = mixing(flux_mix[2], inner_cells(right_pad))
    return summed + diff_span(left_in) * mixed_adj - diff_span(left_in * mixed_adj)


def cell_weight(cell_type):
    return jnp.where(cell_type == 0, 1.0, jnp.where(cell_type == 1, 0.5, 0.0)).astype(jnp.float32)


def per_device(direct_modes, adjoint_modes, base_flow, cell_type, mode_pick, flux_mix):
    modes_count = direct_modes.shape[0]
    cells_all = direct_modes[0].size * lax.axis_size("chord") * lax.axis_size("normal")
    local_sums = jnp.sum(jnp.square(direct_modes.astype(jnp.float32)), axis=(1, 2, 3, 4))
    energy = lax.psum(local_sums, ("chord", "normal")) / cells_all
    amplitude = lax.rsqrt(energy + 1e-06)
    zeros_field = jnp.zeros(base_flow.shape, jnp.float32)
    direct_pad, adjoint_pad = (
        with_halo(direct_modes, (("chord", 2), ("normal", 3)), 1),
        with_halo(adjoint_modes, (("chord", 2), ("normal", 3)), 1),
    )

    def accumulate(number, summed):
        direct = direct_pad[number].astype(jnp.float32)
        adjoint = adjoint_pad[mode_pick[number]].astype(jnp.float32)
        return summed + amplitude[number] * bilinear_term(direct, adjoint, flux_mix)

    gradient = lax.fori_loop(0, modes_count, accumulate, zeros_field) / modes_count
    weight = cell_weight(cell_type)
    base_pad = with_halo(base_flow, (("chord", 1), ("normal", 2)), 1)

    def transpose_step(field_in):
        weighted = with_halo(weight * field_in, (("chord", 1), ("normal", 2)), 1)
        return bilinear_term(base_pad, weighted, flux_mix)

    once_applied = transpose_step(gradient)
    twice_applied = transpose_step(once_applied)
    return twice_applied


def solution(mesh):
    return jax.shard_map(
        per_device,
        mesh=mesh,
        in_specs=(
            P(None, None, "chord", "normal", None),
            P(None, None, "chord", "normal", None),
            P(None, "chord", "normal", None),
            P("chord", "normal", None),
            P(),
            P(),
        ),
        out_specs=P(None, "chord", "normal", None),
        check_vma=False,
    )
```

profile of v0, /device:TPU:121, one launch (start us, length us, event | category | flops | bytes accessed | tf_op | source)
XLA Modules:
  0.0 950.2 jit_solution(10213477555009542439)
XLA Ops:
  21.3 6.3 multiply_reduce_fusion
  31.0 62.0 %psum.7 = f32[16]{0:T(128)S(1)} all-reduce(f32[16]{0:T(128)S(1)} %multiply_reduce_fusion), channel_id=1, replica_groups=mesh['chord'=4,'normal'=32] {'chord','normal'}, use_global_device_ids=true, to_apply=%region_1.0 | all-reduce | flops 16 | bytes 128 | tf_op jit(solution)/shard_map/psum | solution.py:62
  100.5 19.8 %copy_dynamic-update-slice_fusion = bf16[16,5,18,16,256]{4,0,3,2,1:T(8,128)(2,1)} fusion(bf16[16,5,18,16,256]{4,0,3,2,1:T(8,128)(2,1)} %copy_dynamic-update-slice_fusion.4, bf16[16,5,16,16,256]{4,3,2,1,0:T(8,128)(2,1)} %param.9), kind=kLoop, calls=%fused_computation.41 | loop fusion | bytes 20971520
  124.0 6.3 collective-permute-start.8
  134.4 19.5 %copy_dynamic-update-slice_fusion.1 = bf16[16,5,18,16,256]{4,0,3,2,1:T(8,128)(2,1)} fusion(bf16[16,5,18,16,256]{4,0,3,2,1:T(8,128)(2,1)} %copy_dynamic-update-slice_fusion.6, bf16[16,5,16,16,256]{4,3,2,1,0:T(8,128)(2,1)} %param.8), kind=kLoop, calls=%fused_computation.42 | loop fusion | bytes 20971520
  157.5 9.1 collective-permute-start.4
  168.6 7.8 pad_maximum_fusion.1
  176.4 13.5 %copy.52 = bf16[16,5,18,18,256]{4,1,3,2,0:T(8,128)(2,1)} copy(bf16[16,5,18,18,256]{4,0,3,2,1:T(8,128)(2,1)S(1)} %pad_maximum_fusion.1) | data formatting | bytes 26542080
  193.9 13.6 %copy.51 = bf16[16,5,18,18,256]{4,1,3,2,0:T(8,128)(2,1)} copy(bf16[16,5,18,18,256]{4,0,3,2,1:T(8,128)(2,1)S(1)} %pad_maximum_fusion) | data formatting | bytes 26542080
  207.5 629.3 %while.14 = (s32[]{:T(128)}, f32[5,16,16,256]{3,0,2,1:T(8,128)}, f32[16]{0:T(128)S(1)}, bf16[16,5,18,18,256]{4,1,3,2,0:T(8,128)(2,1)}, s32[16]{0:T(128)S(1)}, /*...) while((s32[]{:T(128)}, f32[5,16,16,256]{3,0,2,1:T(8,128)}, ...), condition=%wide.region_3.4_spmd.clone, body=%wide.region_2.3_spmd.clone.sunk | while | flops 78295040 | bytes 61221592 | solution.py:75
  225.1 7.6 convert_multiply_fusion.3
  233.4 12.8 %fusion.76 = f32[5,16,16,256]{3,0,2,1:T(8,128)} fusion(f32[5,18,18,256]{3,0,2,1:T(8,128)} %get-tuple-element.300, f32[5,18,18,256]{3,0,2,1:T(8,128)} %copy-done, f32[5,18,18,256]{3,0,2,1:T(8,128)S(1)} %bitcast_convert_fusion.2, f32[5,18,18,256]{3,0,2,1:T(8,128)} %get-tuple-element.301, f32[5,18,18,256]{3,0,2,1:T(8,128)} %get-tuple-element.302, ...), kind=kLoop, calls=%fused_computation.6.clone.1 | loop fusion | flops 6881280 | bytes 22282244 | tf_op jit(solution)/shard_map/while/body/eval_jaxpr/add | solution.py:73
  263.9 7.6 convert_multiply_fusion.3
  272.1 13.4 %fusion.76 = f32[5,16,16,256]{3,0,2,1:T(8,128)} fusion(f32[5,18,18,256]{3,0,2,1:T(8,128)} %get-tuple-element.300, f32[5,18,18,256]{3,0,2,1:T(8,128)} %copy-done, f32[5,18,18,256]{3,0,2,1:T(8,128)S(1)} %bitcast_convert_fusion.2, f32[5,18,18,256]{3,0,2,1:T(8,128)} %get-tuple-element.301, f32[5,18,18,256]{3,0,2,1:T(8,128)} %get-tuple-element.302, ...), kind=kLoop, calls=%fused_computation.6.clone.1 | loop fusion | flops 6881280 | bytes 22282244 | tf_op jit(solution)/shard_map/while/body/eval_jaxpr/add | solution.py:73
  303.2 7.6 convert_multiply_fusion.3
  311.5 13.4 %fusion.76 = f32[5,16,16,256]{3,0,2,1:T(8,128)} fusion(f32[5,18,18,256]{3,0,2,1:T(8,128)} %get-tuple-element.300, f32[5,18,18,256]{3,0,2,1:T(8,128)} %copy-done, f32[5,18,18,256]{3,0,2,1:T(8,128)S(1)} %bitcast_convert_fusion.2, f32[5,18,18,256]{3,0,2,1:T(8,128)} %get-tuple-element.301, f32[5,18,18,256]{3,0,2,1:T(8,128)} %get-tuple-element.302, ...), kind=kLoop, calls=%fused_computation.6.clone.1 | loop fusion | flops 6881280 | bytes 22282244 | tf_op jit(solution)/shard_map/while/body/eval_jaxpr/add | solution.py:73
  342.6 7.6 convert_multiply_fusion.3
  350.9 13.4 %fusion.76 = f32[5,16,16,256]{3,0,2,1:T(8,128)} fusion(f32[5,18,18,256]{3,0,2,1:T(8,128)} %get-tuple-element.300, f32[5,18,18,256]{3,0,2,1:T(8,128)} %copy-done, f32[5,18,18,256]{3,0,2,1:T(8,128)S(1)} %bitcast_convert_fusion.2, f32[5,18,18,256]{3,0,2,1:T(8,128)} %get-tuple-element.301, f32[5,18,18,256]{3,0,2,1:T(8,128)} %get-tuple-element.302, ...), kind=kLoop, calls=%fused_computation.6.clone.1 | loop fusion | flops 6881280 | bytes 22282244 | tf_op jit(solution)/shard_map/while/body/eval_jaxpr/add | solution.py:73
  381.9 7.6 convert_multiply_fusion.3
  390.2 13.4 %fusion.76 = f32[5,16,16,256]{3,0,2,1:T(8,128)} fusion(f32[5,18,18,256]{3,0,2,1:T(8,128)} %get-tuple-element.300, f32[5,18,18,256]{3,0,2,1:T(8,128)} %copy-done, f32[5,18,18,256]{3,0,2,1:T(8,128)S(1)} %bitcast_convert_fusion.2, f32[5,18,18,256]{3,0,2,1:T(8,128)} %get-tuple-element.301, f32[5,18,18,256]{3,0,2,1:T(8,128)} %get-tuple-element.302, ...), kind=kLoop, calls=%fused_computation.6.clone.1 | loop fusion | flops 6881280 | bytes 22282244 | tf_op jit(solution)/shard_map/while/body/eval_jaxpr/add | solution.py:73
  421.3 7.6 convert_multiply_fusion.3
  429.6 13.4 %fusion.76 = f32[5,16,16,256]{3,0,2,1:T(8,128)} fusion(f32[5,18,18,256]{3,0,2,1:T(8,128)} %get-tuple-element.300, f32[5,18,18,256]{3,0,2,1:T(8,128)} %copy-done, f32[5,18,18,256]{3,0,2,1:T(8,128)S(1)} %bitcast_convert_fusion.2, f32[5,18,18,256]{3,0,2,1:T(8,128)} %get-tuple-element.301, f32[5,18,18,256]{3,0,2,1:T(8,128)} %get-tuple-element.302, ...), kind=kLoop, calls=%fused_computation.6.clone.1 | loop fusion | flops 6881280 | bytes 22282244 | tf_op jit(solution)/shard_map/while/body/eval_jaxpr/add | solution.py:73
  460.7 7.6 convert_multiply_fusion.3
  468.9 13.4 %fusion.76 = f32[5,16,16,256]{3,0,2,1:T(8,128)} fusion(f32[5,18,18,256]{3,0,2,1:T(8,128)} %get-tuple-element.300, f32[5,18,18,256]{3,0,2,1:T(8,128)} %copy-done, f32[5,18,18,256]{3,0,2,1:T(8,128)S(1)} %bitcast_convert_fusion.2, f32[5,18,18,256]{3,0,2,1:T(8,128)} %get-tuple-element.301, f32[5,18,18,256]{3,0,2,1:T(8,128)} %get-tuple-element.302, ...), kind=kLoop, calls=%fused_computation.6.clone.1 | loop fusion | flops 6881280 | bytes 22282244 | tf_op jit(solution)/shard_map/while/body/eval_jaxpr/add | solution.py:73
  500.0 7.6 convert_multiply_fusion.3
  508.3 13.4 %fusion.76 = f32[5,16,16,256]{3,0,2,1:T(8,128)} fusion(f32[5,18,18,256]{3,0,2,1:T(8,128)} %get-tuple-element.300, f32[5,18,18,256]{3,0,2,1:T(8,128)} %copy-done, f32[5,18,18,256]{3,0,2,1:T(8,128)S(1)} %bitcast_convert_fusion.2, f32[5,18,18,256]{3,0,2,1:T(8,128)} %get-tuple-element.301, f32[5,18,18,256]{3,0,2,1:T(8,128)} %get-tuple-element.302, ...), kind=kLoop, calls=%fused_computation.6.clone.1 | loop fusion | flops 6881280 | bytes 22282244 | tf_op jit(solution)/shard_map/while/body/eval_jaxpr/add | solution.py:73
  539.4 7.6 convert_multiply_fusion.3
  547.7 13.4 %fusion.76 = f32[5,16,16,256]{3,0,2,1:T(8,128)} fusion(f32[5,18,18,256]{3,0,2,1:T(8,128)} %get-tuple-element.300, f32[5,18,18,256]{3,0,2,1:T(8,128)} %copy-done, f32[5,18,18,256]{3,0,2,1:T(8,128)S(1)} %bitcast_convert_fusion.2, f32[5,18,18,256]{3,0,2,1:T(8,128)} %get-tuple-element.301, f32[5,18,18,256]{3,0,2,1:T(8,128)} %get-tuple-element.302, ...), kind=kLoop, calls=%fused_computation.6.clone.1 | loop fusion | flops 6881280 | bytes 22282244 | tf_op jit(solution)/shard_map/while/body/eval_jaxpr/add | solution.py:73
  578.7 7.6 convert_multiply_fusion.3
  587.0 13.4 %fusion.76 = f32[5,16,16,256]{3,0,2,1:T(8,128)} fusion(f32[5,18,18,256]{3,0,2,1:T(8,128)} %get-tuple-element.300, f32[5,18,18,256]{3,0,2,1:T(8,128)} %copy-done, f32[5,18,18,256]{3,0,2,1:T(8,128)S(1)} %bitcast_convert_fusion.2, f32[5,18,18,256]{3,0,2,1:T(8,128)} %get-tuple-element.301, f32[5,18,18,256]{3,0,2,1:T(8,128)} %get-tuple-element.302, ...), kind=kLoop, calls=%fused_computation.6.clone.1 | loop fusion | flops 6881280 | bytes 22282244 | tf_op jit(solution)/shard_map/while/body/eval_jaxpr/add | solution.py:73
  618.1 7.6 convert_multiply_fusion.3
  626.4 13.4 %fusion.76 = f32[5,16,16,256]{3,0,2,1:T(8,128)} fusion(f32[5,18,18,256]{3,0,2,1:T(8,128)} %get-tuple-element.300, f32[5,18,18,256]{3,0,2,1:T(8,128)} %copy-done, f32[5,18,18,256]{3,0,2,1:T(8,128)S(1)} %bitcast_convert_fusion.2, f32[5,18,18,256]{3,0,2,1:T(8,128)} %get-tuple-element.301, f32[5,18,18,256]{3,0,2,1:T(8,128)} %get-tuple-element.302, ...), kind=kLoop, calls=%fused_computation.6.clone.1 | loop fusion | flops 6881280 | bytes 22282244 | tf_op jit(solution)/shard_map/while/body/eval_jaxpr/add | solution.py:73
  657.5 7.6 convert_multiply_fusion.3
  665.7 13.4 %fusion.76 = f32[5,16,16,256]{3,0,2,1:T(8,128)} fusion(f32[5,18,18,256]{3,0,2,1:T(8,128)} %get-tuple-element.300, f32[5,18,18,256]{3,0,2,1:T(8,128)} %copy-done, f32[5,18,18,256]{3,0,2,1:T(8,128)S(1)} %bitcast_convert_fusion.2, f32[5,18,18,256]{3,0,2,1:T(8,128)} %get-tuple-element.301, f32[5,18,18,256]{3,0,2,1:T(8,128)} %get-tuple-element.302, ...), kind=kLoop, calls=%fused_computation.6.clone.1 | loop fusion | flops 6881280 | bytes 22282244 | tf_op jit(solution)/shard_map/while/body/eval_jaxpr/add | solution.py:73
  696.8 7.6 convert_multiply_fusion.3
  705.1 13.4 %fusion.76 = f32[5,16,16,256]{3,0,2,1:T(8,128)} fusion(f32[5,18,18,256]{3,0,2,1:T(8,128)} %get-tuple-element.300, f32[5,18,18,256]{3,0,2,1:T(8,128)} %copy-done, f32[5,18,18,256]{3,0,2,1:T(8,128)S(1)} %bitcast_convert_fusion.2, f32[5,18,18,256]{3,0,2,1:T(8,128)} %get-tuple-element.301, f32[5,18,18,256]{3,0,2,1:T(8,128)} %get-tuple-element.302, ...), kind=kLoop, calls=%fused_computation.6.clone.1 | loop fusion | flops 6881280 | bytes 22282244 | tf_op jit(solution)/shard_map/while/body/eval_jaxpr/add | solution.py:73
  736.2 7.6 convert_multiply_fusion.3
  744.5 13.4 %fusion.76 = f32[5,16,16,256]{3,0,2,1:T(8,128)} fusion(f32[5,18,18,256]{3,0,2,1:T(8,128)} %get-tuple-element.300, f32[5,18,18,256]{3,0,2,1:T(8,128)} %copy-done, f32[5,18,18,256]{3,0,2,1:T(8,128)S(1)} %bitcast_convert_fusion.2, f32[5,18,18,256]{3,0,2,1:T(8,128)} %get-tuple-element.301, f32[5,18,18,256]{3,0,2,1:T(8,128)} %get-tuple-element.302, ...), kind=kLoop, calls=%fused_computation.6.clone.1 | loop fusion | flops 6881280 | bytes 22282244 | tf_op jit(solution)/shard_map/while/body/eval_jaxpr/add | solution.py:73
  775.5 7.6 convert_multiply_fusion.3
  783.8 13.4 %fusion.76 = f32[5,16,16,256]{3,0,2,1:T(8,128)} fusion(f32[5,18,18,256]{3,0,2,1:T(8,128)} %get-tuple-element.300, f32[5,18,18,256]{3,0,2,1:T(8,128)} %copy-done, f32[5,18,18,256]{3,0,2,1:T(8,128)S(1)} %bitcast_convert_fusion.2, f32[5,18,18,256]{3,0,2,1:T(8,128)} %get-tuple-element.301, f32[5,18,18,256]{3,0,2,1:T(8,128)} %get-tuple-element.302, ...), kind=kLoop, calls=%fused_computation.6.clone.1 | loop fusion | flops 6881280 | bytes 22282244 | tf_op jit(solution)/shard_map/while/body/eval_jaxpr/add | solution.py:73
  814.9 7.6 convert_multiply_fusion.3
  823.2 13.4 %fusion.76 = f32[5,16,16,256]{3,0,2,1:T(8,128)} fusion(f32[5,18,18,256]{3,0,2,1:T(8,128)} %get-tuple-element.300, f32[5,18,18,256]{3,0,2,1:T(8,128)} %copy-done, f32[5,18,18,256]{3,0,2,1:T(8,128)S(1)} %bitcast_convert_fusion.2, f32[5,18,18,256]{3,0,2,1:T(8,128)} %get-tuple-element.301, f32[5,18,18,256]{3,0,2,1:T(8,128)} %get-tuple-element.302, ...), kind=kLoop, calls=%fused_computation.6.clone.1 | loop fusion | flops 6881280 | bytes 22282244 | tf_op jit(solution)/shard_map/while/body/eval_jaxpr/add | solution.py:73
  858.4 7.1 collective-permute-start.12
  867.4 9.1 collective-permute-start.14
  881.1 7.1 collective-permute-done.15
  893.6 9.5 %fusion.32 = f32[5,16,16,256]{3,0,2,1:T(8,128)S(1)} fusion(f32[5,18,18,256]{3,0,2,1:T(8,128)} %get-tuple-element.210, f32[5,18,18,256]{3,0,2,1:T(8,128)} %copy-done.10, f32[5,18,18,256]{3,0,2,1:T(8,128)} %get-tuple-element.209, f32[5,18,18,256]{3,0,2,1:T(8,128)} %get-tuple-element.240, f32[5,16,16,1]{3,0,2,1:T(8,128)} %get-tuple-element.228, ...), kind=kLoop, calls=%fused_computation.59 | loop fusion | flops 7536640 | bytes 19124224 | tf_op jit(solution)/shard_map/mul | solution.py:80
  922.6 9.1 collective-permute-done.19
  939.6 8.6 fusion.26
  (255 shorter events, 372.4 us)
Async XLA Ops:
  0.0 16.0 %copy-start.4 = (f32[5,16,16,256]{3,2,1,0:T(8,128)S(1)}, f32[5,16,16,256]{3,2,1,0:T(8,128)}, u32[]{:S(2)}) copy-start(f32[5,16,16,256]{3,2,1,0:T(8,128)} %param.10) | copy-start | bytes 3932164
  2.3 96.0 %collective-permute-start.6 = (bf16[16,5,1,16,256]{4,3,2,1,0:T(8,128)(2,1)}, bf16[16,5,1,16,256]{4,3,2,1,0:T(8,128)(2,1)}, u32[]{:S(2)}, u32[]{:S(2)}) collective-permute-start(bf16[16,5,1,16,256]{4,3,2,1,0:T(8,128)(2,1)} %get-tuple-element.204), channel_id=1, source_target_pairs={{0,32},{32,64},{64,96},{1,33},{33,65},{65,97},{2,34},{34,66},{66,9... | collective-permute-start | bytes 1966088 | tf_op jit(solution)/shard_map/ppermute | solution.py:15
  6.0 114.3 %collective-permute-start.7 = (bf16[16,5,1,16,256]{4,3,2,1,0:T(8,128)(2,1)S(1)}, bf16[16,5,1,16,256]{4,3,2,1,0:T(8,128)(2,1)}, u32[]{:S(2)}, u32[]{:S(2)}) collective-permute-start(bf16[16,5,1,16,256]{4,3,2,1,0:T(8,128)(2,1)S(1)} %get-tuple-element.203), channel_id=1, source_target_pairs={{32,0},{64,32},{96,64},{33,1},{65,33},{97,65},{34,2},{66,34},{98,6... | collective-permute-start | bytes 1966088 | tf_op jit(solution)/shard_map/ppermute | solution.py:17
  10.4 121.8 %collective-permute-start.2 = (bf16[16,5,1,16,256]{4,3,2,1,0:T(8,128)(2,1)}, bf16[16,5,1,16,256]{4,3,2,1,0:T(8,128)(2,1)}, u32[]{:S(2)}, u32[]{:S(2)}) collective-permute-start(bf16[16,5,1,16,256]{4,3,2,1,0:T(8,128)(2,1)} %get-tuple-element.206), channel_id=1, source_target_pairs={{0,32},{32,64},{64,96},{1,33},{33,65},{65,97},{2,34},{34,66},{66,9... | collective-permute-start | bytes 1966088 | tf_op jit(solution)/shard_map/ppermute | solution.py:15
  14.1 139.8 %collective-permute-start.3 = (bf16[16,5,1,16,256]{4,3,2,1,0:T(8,128)(2,1)}, bf16[16,5,1,16,256]{4,3,2,1,0:T(8,128)(2,1)}, u32[]{:S(2)}, u32[]{:S(2)}) collective-permute-start(bf16[16,5,1,16,256]{4,3,2,1,0:T(8,128)(2,1)} %get-tuple-element.205), channel_id=1, source_target_pairs={{32,0},{64,32},{96,64},{33,1},{65,33},{97,65},{34,2},{66,34},{98,6... | collective-permute-start | bytes 1966088 | tf_op jit(solution)/shard_map/ppermute | solution.py:17
  16.9 76.2 %copy-start.1 = (f32[5,16,16,256]{3,0,2,1:T(8,128)}, f32[5,16,16,256]{3,0,2,1:T(8,128)S(1)}, u32[]{:S(2)}) copy-start(f32[5,16,16,256]{3,0,2,1:T(8,128)S(1)} %copy.42) | copy-start | bytes 3932164
  17.6 77.2 %collective-permute-start.1 = (f32[5,1,16,256]{3,0,2,1:T(8,128)S(1)}, f32[5,1,16,256]{3,0,2,1:T(8,128)S(1)}, u32[]{:S(2)}, u32[]{:S(2)}) collective-permute-start(f32[5,1,16,256]{3,0,2,1:T(8,128)S(1)} %get-tuple-element.232), channel_id=1, source_target_pairs={{0,32},{32,64},{64,96},{1,33},{33,65},{65,97},{2,34},{34,66},{66,9... | collective-permute-start | bytes 245768 | tf_op jit(solution)/shard_map/ppermute | solution.py:15
  94.8 25.5 %copy-start.12 = (f32[5,1,16,256]{3,0,2,1:T(8,128)}, f32[5,1,16,256]{3,0,2,1:T(8,128)S(1)}, u32[]{:S(2)}) copy-start(f32[5,1,16,256]{3,0,2,1:T(8,128)S(1)} %collective-permute-done.1) | copy-start | bytes 245764
  94.8 759.2 %collective-permute-start = (f32[5,1,16,256]{3,0,2,1:T(8,128)}, f32[5,1,16,256]{3,0,2,1:T(8,128)}, u32[]{:S(2)}, u32[]{:S(2)}) collective-permute-start(f32[5,1,16,256]{3,0,2,1:T(8,128)} %get-tuple-element.231), channel_id=1, source_target_pairs={{32,0},{64,32},{96,64},{33,1},{65,33},{97,65},{34,2},{66,34},{98,6... | collective-permute-start | bytes 245768 | tf_op jit(solution)/shard_map/ppermute | solution.py:17
  124.0 44.6 %collective-permute-start.8 = (bf16[16,5,18,1,256]{4,0,3,2,1:T(8,128)(2,1)S(1)}, bf16[16,5,18,1,256]{4,0,3,2,1:T(8,128)(2,1)S(1)}, u32[]{:S(2)}, u32[]{:S(2)}) collective-permute-start(bf16[16,5,18,1,256]{4,0,3,2,1:T(8,128)(2,1)S(1)} %get-tuple-element.199), channel_id=1, source_target_pairs={{0,1},{1,2},{2,3},{3,4},{4,5},{5,6},{6,7},{7,8},{8,9},{9,10},{10,1... | collective-permute-start | bytes 2211848 | tf_op jit(solution)/shard_map/ppermute | solution.py:15
  130.3 38.3 %collective-permute-start.9 = (bf16[16,5,18,1,256]{4,0,3,2,1:T(8,128)(2,1)S(1)}, bf16[16,5,18,1,256]{4,0,3,2,1:T(8,128)(2,1)S(1)}, u32[]{:S(2)}, u32[]{:S(2)}) collective-permute-start(bf16[16,5,18,1,256]{4,0,3,2,1:T(8,128)(2,1)S(1)} %get-tuple-element.200), channel_id=1, source_target_pairs={{1,0},{2,1},{3,2},{4,3},{5,4},{6,5},{7,6},{8,7},{9,8},{10,9},{11,1... | collective-permute-start | bytes 2211848 | tf_op jit(solution)/shard_map/ppermute | solution.py:17
  157.5 32.4 %collective-permute-start.4 = (bf16[16,5,18,1,256]{4,0,3,2,1:T(8,128)(2,1)S(1)}, bf16[16,5,18,1,256]{4,0,3,2,1:T(8,128)(2,1)S(1)}, u32[]{:S(2)}, u32[]{:S(2)}) collective-permute-start(bf16[16,5,18,1,256]{4,0,3,2,1:T(8,128)(2,1)S(1)} %get-tuple-element.201), channel_id=1, source_target_pairs={{0,1},{1,2},{2,3},{3,4},{4,5},{5,6},{6,7},{7,8},{8,9},{9,10},{10,1... | collective-permute-start | bytes 2211848 | tf_op jit(solution)/shard_map/ppermute | solution.py:15
  166.6 25.5 %collective-permute-start.5 = (bf16[16,5,18,1,256]{4,0,3,2,1:T(8,128)(2,1)S(1)}, bf16[16,5,18,1,256]{4,0,3,2,1:T(8,128)(2,1)S(1)}, u32[]{:S(2)}, u32[]{:S(2)}) collective-permute-start(bf16[16,5,18,1,256]{4,0,3,2,1:T(8,128)(2,1)S(1)} %get-tuple-element.202), channel_id=1, source_target_pairs={{1,0},{2,1},{3,2},{4,3},{5,4},{6,5},{7,6},{8,7},{9,8},{10,9},{11,1... | collective-permute-start | bytes 2211848 | tf_op jit(solution)/shard_map/ppermute | solution.py:17
  168.6 23.5 %slice-start = ((s8[11796480]{0:T(1024)(128)(4,1)}), s8[4194304]{0:T(1024)(128)(4,1)S(1)}, s32[]{:S(2)}) async-start(s8[11796480]{0:T(1024)(128)(4,1)} %bitcast.119), calls=%async_computation | async-start | bytes 8388608
  168.6 23.5 %slice-start.1 = ((s8[11796480]{0:T(1024)(128)(4,1)}), s8[4194304]{0:T(1024)(128)(4,1)S(1)}, s32[]{:S(2)}) async-start(s8[11796480]{0:T(1024)(128)(4,1)} %bitcast.119), calls=%async_computation.1 | async-start | bytes 8388608
  176.4 15.7 %slice-start.2 = ((s8[11796480]{0:T(1024)(128)(4,1)}), s8[3407872]{0:T(1024)(128)(4,1)S(1)}, s32[]{:S(2)}) async-start(s8[11796480]{0:T(1024)(128)(4,1)} %bitcast.119), calls=%async_computation.2 | async-start | bytes 6815744
  193.9 13.6 %copy-start.17 = (s32[16]{0:T(128)S(1)}, s32[16]{0:T(128)}, u32[]{:S(2)}) copy-start(s32[16]{0:T(128)} %param.12) | copy-start | bytes 196
  207.5 629.4 %copy-start.14 = (f32[16,16,256]{2,1,0:T(8,128)S(1)}, f32[16,16,256]{2,1,0:T(8,128)}, u32[]{:S(2)}) copy-start(f32[16,16,256]{2,1,0:T(8,128)} %get-tuple-element.238) | copy-start | bytes 786436
  303.2 7.6 copy-start
  342.6 7.6 copy-start
  381.9 7.6 copy-start
  421.3 7.6 copy-start
  460.6 7.6 copy-start
  500.0 7.6 copy-start
  539.4 7.6 copy-start
  578.7 7.6 copy-start
  618.1 7.6 copy-start
  657.4 7.6 copy-start
  696.8 7.6 copy-start
  736.2 7.6 copy-start
  775.5 7.6 copy-start
  848.0 7.0 collective-permute-start.10
  852.1 6.3 collective-permute-start.11
  858.4 20.1 %collective-permute-start.12 = (f32[5,18,1,256]{3,0,2,1:T(8,128)S(1)}, f32[5,18,1,256]{3,0,2,1:T(8,128)S(1)}, u32[]{:S(2)}, u32[]{:S(2)}) collective-permute-start(f32[5,18,1,256]{3,0,2,1:T(8,128)S(1)} %get-tuple-element.215), channel_id=1, source_target_pairs={{0,1},{1,2},{2,3},{3,4},{4,5},{5,6},{6,7},{7,8},{8,9},{9,10},{10,1... | collective-permute-start | bytes 276488 | tf_op jit(solution)/shard_map/ppermute | solution.py:15
  865.5 13.0 %collective-permute-start.13 = (f32[5,18,1,256]{3,0,2,1:T(8,128)S(1)}, f32[5,18,1,256]{3,0,2,1:T(8,128)S(1)}, u32[]{:S(2)}, u32[]{:S(2)}) collective-permute-start(f32[5,18,1,256]{3,0,2,1:T(8,128)S(1)} %get-tuple-element.216), channel_id=1, source_target_pairs={{1,0},{2,1},{3,2},{4,3},{5,4},{6,5},{7,6},{8,7},{9,8},{10,9},{11,1... | collective-permute-start | bytes 276488 | tf_op jit(solution)/shard_map/ppermute | solution.py:17
  867.4 13.6 %collective-permute-start.14 = (f32[5,18,1,256]{3,0,2,1:T(8,128)S(1)}, f32[5,18,1,256]{3,0,2,1:T(8,128)S(1)}, u32[]{:S(2)}, u32[]{:S(2)}) collective-permute-start(f32[5,18,1,256]{3,0,2,1:T(8,128)S(1)} %get-tuple-element.213), channel_id=1, source_target_pairs={{0,1},{1,2},{2,3},{3,4},{4,5},{5,6},{6,7},{7,8},{8,9},{9,10},{10,1... | collective-permute-start | bytes 276488 | tf_op jit(solution)/shard_map/ppermute | solution.py:15
  876.5 11.6 %collective-permute-start.15 = (f32[5,18,1,256]{3,0,2,1:T(8,128)S(1)}, f32[5,18,1,256]{3,0,2,1:T(8,128)S(1)}, u32[]{:S(2)}, u32[]{:S(2)}) collective-permute-start(f32[5,18,1,256]{3,0,2,1:T(8,128)S(1)} %get-tuple-element.214), channel_id=1, source_target_pairs={{1,0},{2,1},{3,2},{4,3},{5,4},{6,5},{7,6},{8,7},{9,8},{10,9},{11,1... | collective-permute-start | bytes 276488 | tf_op jit(solution)/shard_map/ppermute | solution.py:17
  881.0 12.6 %copy-start.10 = (f32[5,18,18,256]{3,0,2,1:T(8,128)}, f32[5,18,18,256]{3,0,2,1:T(8,128)S(1)}, u32[]{:S(2)}) copy-start(f32[5,18,18,256]{3,0,2,1:T(8,128)S(1)} %convolution_bitcast_fusion.4) | copy-start | bytes 4976644
  881.0 12.6 %copy-start.2 = (f32[5,16,16,256]{3,0,2,1:T(8,128)S(1)}, f32[5,16,16,256]{3,0,2,1:T(8,128)}, u32[]{:S(2)}) copy-start(f32[5,16,16,256]{3,0,2,1:T(8,128)} %copy-done.1) | copy-start | bytes 3932164
  881.0 12.5 %copy-start.6 = (f32[5,16,16,255]{3,0,2,1:T(8,128)S(1)}, f32[5,16,16,255]{3,0,2,1:T(8,128)}, u32[]{:S(2)}) copy-start(f32[5,16,16,255]{3,0,2,1:T(8,128)} %get-tuple-element.223) | copy-start | bytes 3916804
  881.0 12.5 %copy-start.7 = (f32[5,16,16,255]{3,0,2,1:T(8,128)S(1)}, f32[5,16,16,255]{3,0,2,1:T(8,128)}, u32[]{:S(2)}) copy-start(f32[5,16,16,255]{3,0,2,1:T(8,128)} %get-tuple-element.224) | copy-start | bytes 3916804
  881.0 12.5 %copy-start.8 = (f32[5,16,16,1]{3,0,2,1:T(8,128)S(1)}, f32[5,16,16,1]{3,0,2,1:T(8,128)}, u32[]{:S(2)}) copy-start(f32[5,16,16,1]{3,0,2,1:T(8,128)} %get-tuple-element.225) | copy-start | bytes 15364
  881.0 12.5 %copy-start.9 = (f32[5,16,16,1]{3,0,2,1:T(8,128)S(1)}, f32[5,16,16,1]{3,0,2,1:T(8,128)}, u32[]{:S(2)}) copy-start(f32[5,16,16,1]{3,0,2,1:T(8,128)} %get-tuple-element.226) | copy-start | bytes 15364
  881.0 12.5 %copy-start.13 = (f32[5,1,16,256]{3,0,2,1:T(8,128)S(1)}, f32[5,1,16,256]{3,0,2,1:T(8,128)}, u32[]{:S(2)}) copy-start(f32[5,1,16,256]{3,0,2,1:T(8,128)} %copy-done.12) | copy-start | bytes 245764
  907.2 7.8 collective-permute-start.16
  910.4 6.3 collective-permute-start.17
  916.7 5.9 collective-permute-start.18
  920.1 11.6 %collective-permute-start.19 = (f32[5,18,1,256]{3,0,2,1:T(8,128)S(1)}, f32[5,18,1,256]{3,0,2,1:T(8,128)S(1)}, u32[]{:S(2)}, u32[]{:S(2)}) collective-permute-start(f32[5,18,1,256]{3,0,2,1:T(8,128)S(1)} %get-tuple-element.212), channel_id=1, source_target_pairs={{1,0},{2,1},{3,2},{4,3},{5,4},{6,5},{7,6},{8,7},{9,8},{10,9},{11,1... | collective-permute-start | bytes 276488 | tf_op jit(solution)/shard_map/ppermute | solution.py:17
  (8 other events, 37.7 us)
where the time goes:
time: 959 us; the launch traced here: 950 us
  other arithmetic  277 us (29%)
  matrix products  247 us (26%)
  local copies, waits for them, and re-layouts  235 us (25%)
  starting transfers between devices  73.2 us (8%)
  blocking collectives  62 us (6%)
  loops' own time  32 us (3%)
  waiting for transfers between devices  23.7 us (2%)
    dot_general x54, matrix products, mixing(): jnp.einsum('ij,i...->j...', matrix, field_in, precision=lax.Precision.HIG...  247 us
    add x16, other arithmetic, accumulate(): return summed + amplitude[number] * bilinear_term(direct, adjoint, flux_mix)  214 us
    slice x38, local copies, waits for them, and re-layouts, diff_span(): return jnp.roll(field_in, -1, -1) - jnp.roll(field_in, 1, -1)  127 us
    unnamed x49, local copies, waits for them, and re-layouts  73 us
    psum x1, blocking collectives, per_device(): energy = lax.psum(local_sums, ('chord', 'normal')) / cells_all  62 us
    ppermute x10, starting transfers between devices, with_halo(): lax.ppermute(tail, axis, [(i, (i + 1) % count) for i in range(ends)])  53.1 us
    another operation x1, loops' own time, per_device(): lax.fori_loop(0, modes_count, accumulate, zeros_field) / modes_count  32 us
    convert_element_type x16, other arithmetic, accumulate(): direct = direct_pad[number].astype(jnp.float32)  25.6 us
  transfers between devices with their start and end apart: 20, of which 6 were waited for; matrix products, arithmetic and copies ran while one was open for 76% of the time, Pallas kernels for 0%

commit v1 on v0

--- a/solution.py
+++ b/solution.py
@@ -2,6 +2,12 @@
 import jax.numpy as jnp
 from jax import lax
 from jax.sharding import PartitionSpec as P
+
+
+def push_ranges(unit, mesh_name, bus_axis):
+    for k in (mesh_name, bus_axis):
+        unit = lax.psum(unit, k)
+    return unit
 
 
 def with_halo(cells, sides, width):
@@ -59,7 +65,7 @@
     modes_count = direct_modes.shape[0]
     cells_all = direct_modes[0].size * lax.axis_size("chord") * lax.axis_size("normal")
     local_sums = jnp.sum(jnp.square(direct_modes.astype(jnp.float32)), axis=(1, 2, 3, 4))
-    energy = lax.psum(local_sums, ("chord", "normal")) / cells_all
+    energy = push_ranges(local_sums, "chord", "normal") / cells_all
     amplitude = lax.rsqrt(energy + 1e-06)
     zeros_field = jnp.zeros(base_flow.shape, jnp.float32)
     direct_pad, adjoint_pad = (

time: 959 us -> 995 us (1.038)
  starting transfers between devices: 73.2 us -> 91.4 us
  blocking collectives: 62 us -> 79.8 us
    psum x1 -> x2, blocking collectives: 62 us -> 79.8 us  [push_ranges(): unit = lax.psum(unit, k)]
    ppermute x10, starting transfers between devices: 20.1 us -> 34.4 us  [with_halo(): lax.ppermute(head, axis, [((i + 1) % count, i) for i in range(ends)])]
  transfers between devices with their start and end apart: 20 -> 20, of which waited for: 6 -> 6; matrix products, arithmetic and copies ran while one was open for 76% -> 73% of each run, Pallas kernels for 0% -> 0%
where the time goes in v1:
time: 995 us; the launch traced here: 987 us
  other arithmetic  277 us (28%)
  matrix products  247 us (25%)
  local copies, waits for them, and re-layouts  235 us (24%)
  starting transfers between devices  91.4 us (9%)
  blocking collectives  79.8 us (8%)
  loops' own time  32 us (3%)
  waiting for transfers between devices  23.7 us (2%)
    dot_general x54, matrix products, mixing(): jnp.einsum('ij,i...->j...', matrix, field_in, precision=lax.Precision.HIG...  247 us
    add x16, other arithmetic, accumulate(): return summed + amplitude[number] * bilinear_term(direct, adjoint, flux_mix)  215 us
    slice x38, local copies, waits for them, and re-layouts, diff_span(): return jnp.roll(field_in, -1, -1) - jnp.roll(field_in, 1, -1)  127 us
    psum x2, blocking collectives, push_ranges(): unit = lax.psum(unit, k)  79.8 us
    unnamed x49, local copies, waits for them, and re-layouts  72.9 us
    ppermute x10, starting transfers between devices, with_halo(): lax.ppermute(tail, axis, [(i, (i + 1) % count) for i in range(ends)])  57 us
    ppermute x10, starting transfers between devices, with_halo(): lax.ppermute(head, axis, [((i + 1) % count, i) for i in range(ends)])  34.4 us
    another operation x1, loops' own time, per_device(): lax.fori_loop(0, modes_count, accumulate, zeros_field) / modes_count  32 us
  transfers between devices with their start and end apart: 20, of which 6 were waited for; matrix products, arithmetic and copies ran while one was open for 73% of the time, Pallas kernels for 0%

profile of v1, /device:TPU:121, one launch (start us, length us, event | category | flops | bytes accessed | tf_op | source)
XLA Modules:
  0.0 986.9 jit_solution(4055199788733194019)
XLA Ops:
  36.2 74.7 %psum.15 = f32[16]{0:T(128)S(1)} all-reduce(f32[16]{0:T(128)S(1)} %psum.14), channel_id=1, replica_groups=mesh['chord'=4,'normal'=32] {'normal'}, use_global_device_ids=true, to_apply=%region_2.0 | all-reduce | flops 16 | bytes 128 | tf_op jit(solution)/shard_map/psum | solution.py:9
  112.6 17.1 %collective-permute-start = (f32[5,1,16,256]{3,0,2,1:T(8,128)}, f32[5,1,16,256]{3,0,2,1:T(8,128)}, u32[]{:S(2)}, u32[]{:S(2)}) collective-permute-start(f32[5,1,16,256]{3,0,2,1:T(8,128)} %get-tuple-element.231), channel_id=1, source_target_pairs={{32,0},{64,32},{96,64},{33,1},{65,33},{97,65},{34,2},{66,34},{98,6... | collective-permute-start | bytes 245768 | tf_op jit(solution)/shard_map/ppermute | solution.py:23
  132.5 19.8 %copy_dynamic-update-slice_fusion = bf16[16,5,18,16,256]{4,0,3,2,1:T(8,128)(2,1)} fusion(bf16[16,5,18,16,256]{4,0,3,2,1:T(8,128)(2,1)} %copy_dynamic-update-slice_fusion.4, bf16[16,5,16,16,256]{4,3,2,1,0:T(8,128)(2,1)} %param.9), kind=kLoop, calls=%fused_computation.41 | loop fusion | bytes 20971520
  156.0 9.6 collective-permute-start.8
  169.7 19.5 %copy_dynamic-update-slice_fusion.1 = bf16[16,5,18,16,256]{4,0,3,2,1:T(8,128)(2,1)} fusion(bf16[16,5,18,16,256]{4,0,3,2,1:T(8,128)(2,1)} %copy_dynamic-update-slice_fusion.6, bf16[16,5,16,16,256]{4,3,2,1,0:T(8,128)(2,1)} %param.8), kind=kLoop, calls=%fused_computation.42 | loop fusion | bytes 20971520
  192.8 9.1 collective-permute-start.4
  203.8 7.8 pad_maximum_fusion.1
  211.6 13.5 %copy.52 = bf16[16,5,18,18,256]{4,1,3,2,0:T(8,128)(2,1)} copy(bf16[16,5,18,18,256]{4,0,3,2,1:T(8,128)(2,1)S(1)} %pad_maximum_fusion.1) | data formatting | bytes 26542080
  229.1 13.5 %copy.51 = bf16[16,5,18,18,256]{4,1,3,2,0:T(8,128)(2,1)} copy(bf16[16,5,18,18,256]{4,0,3,2,1:T(8,128)(2,1)S(1)} %pad_maximum_fusion) | data formatting | bytes 26542080
  242.7 630.4 %while.14 = (s32[]{:T(128)}, f32[5,16,16,256]{3,0,2,1:T(8,128)}, f32[16]{0:T(128)S(1)}, bf16[16,5,18,18,256]{4,1,3,2,0:T(8,128)(2,1)}, s32[16]{0:T(128)S(1)}, /*...) while((s32[]{:T(128)}, f32[5,16,16,256]{3,0,2,1:T(8,128)}, ...), condition=%wide.region_4.5_spmd.clone, body=%wide.region_3.4_spmd.clone.sunk | while | flops 78295040 | bytes 61221592 | solution.py:81
  260.3 7.6 convert_multiply_fusion.3
  268.6 12.9 %fusion.76 = f32[5,16,16,256]{3,0,2,1:T(8,128)} fusion(f32[5,18,18,256]{3,0,2,1:T(8,128)} %get-tuple-element.300, f32[5,18,18,256]{3,0,2,1:T(8,128)} %copy-done, f32[5,18,18,256]{3,0,2,1:T(8,128)S(1)} %bitcast_convert_fusion.2, f32[5,18,18,256]{3,0,2,1:T(8,128)} %get-tuple-element.301, f32[5,18,18,256]{3,0,2,1:T(8,128)} %get-tuple-element.302, ...), kind=kLoop, calls=%fused_computation.6.clone.1 | loop fusion | flops 6881280 | bytes 22282244 | tf_op jit(solution)/shard_map/while/body/eval_jaxpr/add | solution.py:79
  299.1 7.6 convert_multiply_fusion.3
  307.4 13.5 %fusion.76 = f32[5,16,16,256]{3,0,2,1:T(8,128)} fusion(f32[5,18,18,256]{3,0,2,1:T(8,128)} %get-tuple-element.300, f32[5,18,18,256]{3,0,2,1:T(8,128)} %copy-done, f32[5,18,18,256]{3,0,2,1:T(8,128)S(1)} %bitcast_convert_fusion.2, f32[5,18,18,256]{3,0,2,1:T(8,128)} %get-tuple-element.301, f32[5,18,18,256]{3,0,2,1:T(8,128)} %get-tuple-element.302, ...), kind=kLoop, calls=%fused_computation.6.clone.1 | loop fusion | flops 6881280 | bytes 22282244 | tf_op jit(solution)/shard_map/while/body/eval_jaxpr/add | solution.py:79
  338.6 7.6 convert_multiply_fusion.3
  346.9 13.5 %fusion.76 = f32[5,16,16,256]{3,0,2,1:T(8,128)} fusion(f32[5,18,18,256]{3,0,2,1:T(8,128)} %get-tuple-element.300, f32[5,18,18,256]{3,0,2,1:T(8,128)} %copy-done, f32[5,18,18,256]{3,0,2,1:T(8,128)S(1)} %bitcast_convert_fusion.2, f32[5,18,18,256]{3,0,2,1:T(8,128)} %get-tuple-element.301, f32[5,18,18,256]{3,0,2,1:T(8,128)} %get-tuple-element.302, ...), kind=kLoop, calls=%fused_computation.6.clone.1 | loop fusion | flops 6881280 | bytes 22282244 | tf_op jit(solution)/shard_map/while/body/eval_jaxpr/add | solution.py:79
  378.0 7.6 convert_multiply_fusion.3
  386.3 13.5 %fusion.76 = f32[5,16,16,256]{3,0,2,1:T(8,128)} fusion(f32[5,18,18,256]{3,0,2,1:T(8,128)} %get-tuple-element.300, f32[5,18,18,256]{3,0,2,1:T(8,128)} %copy-done, f32[5,18,18,256]{3,0,2,1:T(8,128)S(1)} %bitcast_convert_fusion.2, f32[5,18,18,256]{3,0,2,1:T(8,128)} %get-tuple-element.301, f32[5,18,18,256]{3,0,2,1:T(8,128)} %get-tuple-element.302, ...), kind=kLoop, calls=%fused_computation.6.clone.1 | loop fusion | flops 6881280 | bytes 22282244 | tf_op jit(solution)/shard_map/while/body/eval_jaxpr/add | solution.py:79
  417.4 7.6 convert_multiply_fusion.3
  425.7 13.5 %fusion.76 = f32[5,16,16,256]{3,0,2,1:T(8,128)} fusion(f32[5,18,18,256]{3,0,2,1:T(8,128)} %get-tuple-element.300, f32[5,18,18,256]{3,0,2,1:T(8,128)} %copy-done, f32[5,18,18,256]{3,0,2,1:T(8,128)S(1)} %bitcast_convert_fusion.2, f32[5,18,18,256]{3,0,2,1:T(8,128)} %get-tuple-element.301, f32[5,18,18,256]{3,0,2,1:T(8,128)} %get-tuple-element.302, ...), kind=kLoop, calls=%fused_computation.6.clone.1 | loop fusion | flops 6881280 | bytes 22282244 | tf_op jit(solution)/shard_map/while/body/eval_jaxpr/add | solution.py:79
  456.8 7.6 convert_multiply_fusion.3
  465.1 13.5 %fusion.76 = f32[5,16,16,256]{3,0,2,1:T(8,128)} fusion(f32[5,18,18,256]{3,0,2,1:T(8,128)} %get-tuple-element.300, f32[5,18,18,256]{3,0,2,1:T(8,128)} %copy-done, f32[5,18,18,256]{3,0,2,1:T(8,128)S(1)} %bitcast_convert_fusion.2, f32[5,18,18,256]{3,0,2,1:T(8,128)} %get-tuple-element.301, f32[5,18,18,256]{3,0,2,1:T(8,128)} %get-tuple-element.302, ...), kind=kLoop, calls=%fused_computation.6.clone.1 | loop fusion | flops 6881280 | bytes 22282244 | tf_op jit(solution)/shard_map/while/body/eval_jaxpr/add | solution.py:79
  496.3 7.6 convert_multiply_fusion.3
  504.6 13.5 %fusion.76 = f32[5,16,16,256]{3,0,2,1:T(8,128)} fusion(f32[5,18,18,256]{3,0,2,1:T(8,128)} %get-tuple-element.300, f32[5,18,18,256]{3,0,2,1:T(8,128)} %copy-done, f32[5,18,18,256]{3,0,2,1:T(8,128)S(1)} %bitcast_convert_fusion.2, f32[5,18,18,256]{3,0,2,1:T(8,128)} %get-tuple-element.301, f32[5,18,18,256]{3,0,2,1:T(8,128)} %get-tuple-element.302, ...), kind=kLoop, calls=%fused_computation.6.clone.1 | loop fusion | flops 6881280 | bytes 22282244 | tf_op jit(solution)/shard_map/while/body/eval_jaxpr/add | solution.py:79
  535.7 7.6 convert_multiply_fusion.3
  544.0 13.5 %fusion.76 = f32[5,16,16,256]{3,0,2,1:T(8,128)} fusion(f32[5,18,18,256]{3,0,2,1:T(8,128)} %get-tuple-element.300, f32[5,18,18,256]{3,0,2,1:T(8,128)} %copy-done, f32[5,18,18,256]{3,0,2,1:T(8,128)S(1)} %bitcast_convert_fusion.2, f32[5,18,18,256]{3,0,2,1:T(8,128)} %get-tuple-element.301, f32[5,18,18,256]{3,0,2,1:T(8,128)} %get-tuple-element.302, ...), kind=kLoop, calls=%fused_computation.6.clone.1 | loop fusion | flops 6881280 | bytes 22282244 | tf_op jit(solution)/shard_map/while/body/eval_jaxpr/add | solution.py:79
  575.1 7.6 convert_multiply_fusion.3
  583.4 13.5 %fusion.76 = f32[5,16,16,256]{3,0,2,1:T(8,128)} fusion(f32[5,18,18,256]{3,0,2,1:T(8,128)} %get-tuple-element.300, f32[5,18,18,256]{3,0,2,1:T(8,128)} %copy-done, f32[5,18,18,256]{3,0,2,1:T(8,128)S(1)} %bitcast_convert_fusion.2, f32[5,18,18,256]{3,0,2,1:T(8,128)} %get-tuple-element.301, f32[5,18,18,256]{3,0,2,1:T(8,128)} %get-tuple-element.302, ...), kind=kLoop, calls=%fused_computation.6.clone.1 | loop fusion | flops 6881280 | bytes 22282244 | tf_op jit(solution)/shard_map/while/body/eval_jaxpr/add | solution.py:79
  614.6 7.6 convert_multiply_fusion.3
  622.9 13.5 %fusion.76 = f32[5,16,16,256]{3,0,2,1:T(8,128)} fusion(f32[5,18,18,256]{3,0,2,1:T(8,128)} %get-tuple-element.300, f32[5,18,18,256]{3,0,2,1:T(8,128)} %copy-done, f32[5,18,18,256]{3,0,2,1:T(8,128)S(1)} %bitcast_convert_fusion.2, f32[5,18,18,256]{3,0,2,1:T(8,128)} %get-tuple-element.301, f32[5,18,18,256]{3,0,2,1:T(8,128)} %get-tuple-element.302, ...), kind=kLoop, calls=%fused_computation.6.clone.1 | loop fusion | flops 6881280 | bytes 22282244 | tf_op jit(solution)/shard_map/while/body/eval_jaxpr/add | solution.py:79
  654.0 7.6 convert_multiply_fusion.3
  662.3 13.5 %fusion.76 = f32[5,16,16,256]{3,0,2,1:T(8,128)} fusion(f32[5,18,18,256]{3,0,2,1:T(8,128)} %get-tuple-element.300, f32[5,18,18,256]{3,0,2,1:T(8,128)} %copy-done, f32[5,18,18,256]{3,0,2,1:T(8,128)S(1)} %bitcast_convert_fusion.2, f32[5,18,18,256]{3,0,2,1:T(8,128)} %get-tuple-element.301, f32[5,18,18,256]{3,0,2,1:T(8,128)} %get-tuple-element.302, ...), kind=kLoop, calls=%fused_computation.6.clone.1 | loop fusion | flops 6881280 | bytes 22282244 | tf_op jit(solution)/shard_map/while/body/eval_jaxpr/add | solution.py:79
  693.4 7.6 convert_multiply_fusion.3
  701.7 13.5 %fusion.76 = f32[5,16,16,256]{3,0,2,1:T(8,128)} fusion(f32[5,18,18,256]{3,0,2,1:T(8,128)} %get-tuple-element.300, f32[5,18,18,256]{3,0,2,1:T(8,128)} %copy-done, f32[5,18,18,256]{3,0,2,1:T(8,128)S(1)} %bitcast_convert_fusion.2, f32[5,18,18,256]{3,0,2,1:T(8,128)} %get-tuple-element.301, f32[5,18,18,256]{3,0,2,1:T(8,128)} %get-tuple-element.302, ...), kind=kLoop, calls=%fused_computation.6.clone.1 | loop fusion | flops 6881280 | bytes 22282244 | tf_op jit(solution)/shard_map/while/body/eval_jaxpr/add | solution.py:79
  732.8 7.6 convert_multiply_fusion.3
  741.1 13.5 %fusion.76 = f32[5,16,16,256]{3,0,2,1:T(8,128)} fusion(f32[5,18,18,256]{3,0,2,1:T(8,128)} %get-tuple-element.300, f32[5,18,18,256]{3,0,2,1:T(8,128)} %copy-done, f32[5,18,18,256]{3,0,2,1:T(8,128)S(1)} %bitcast_convert_fusion.2, f32[5,18,18,256]{3,0,2,1:T(8,128)} %get-tuple-element.301, f32[5,18,18,256]{3,0,2,1:T(8,128)} %get-tuple-element.302, ...), kind=kLoop, calls=%fused_computation.6.clone.1 | loop fusion | flops 6881280 | bytes 22282244 | tf_op jit(solution)/shard_map/while/body/eval_jaxpr/add | solution.py:79
  772.3 7.6 convert_multiply_fusion.3
  780.6 13.5 %fusion.76 = f32[5,16,16,256]{3,0,2,1:T(8,128)} fusion(f32[5,18,18,256]{3,0,2,1:T(8,128)} %get-tuple-element.300, f32[5,18,18,256]{3,0,2,1:T(8,128)} %copy-done, f32[5,18,18,256]{3,0,2,1:T(8,128)S(1)} %bitcast_convert_fusion.2, f32[5,18,18,256]{3,0,2,1:T(8,128)} %get-tuple-element.301, f32[5,18,18,256]{3,0,2,1:T(8,128)} %get-tuple-element.302, ...), kind=kLoop, calls=%fused_computation.6.clone.1 | loop fusion | flops 6881280 | bytes 22282244 | tf_op jit(solution)/shard_map/while/body/eval_jaxpr/add | solution.py:79
  811.7 7.6 convert_multiply_fusion.3
  820.0 13.5 %fusion.76 = f32[5,16,16,256]{3,0,2,1:T(8,128)} fusion(f32[5,18,18,256]{3,0,2,1:T(8,128)} %get-tuple-element.300, f32[5,18,18,256]{3,0,2,1:T(8,128)} %copy-done, f32[5,18,18,256]{3,0,2,1:T(8,128)S(1)} %bitcast_convert_fusion.2, f32[5,18,18,256]{3,0,2,1:T(8,128)} %get-tuple-element.301, f32[5,18,18,256]{3,0,2,1:T(8,128)} %get-tuple-element.302, ...), kind=kLoop, calls=%fused_computation.6.clone.1 | loop fusion | flops 6881280 | bytes 22282244 | tf_op jit(solution)/shard_map/while/body/eval_jaxpr/add | solution.py:79
  851.1 7.6 convert_multiply_fusion.3
  859.4 13.5 %fusion.76 = f32[5,16,16,256]{3,0,2,1:T(8,128)} fusion(f32[5,18,18,256]{3,0,2,1:T(8,128)} %get-tuple-element.300, f32[5,18,18,256]{3,0,2,1:T(8,128)} %copy-done, f32[5,18,18,256]{3,0,2,1:T(8,128)S(1)} %bitcast_convert_fusion.2, f32[5,18,18,256]{3,0,2,1:T(8,128)} %get-tuple-element.301, f32[5,18,18,256]{3,0,2,1:T(8,128)} %get-tuple-element.302, ...), kind=kLoop, calls=%fused_computation.6.clone.1 | loop fusion | flops 6881280 | bytes 22282244 | tf_op jit(solution)/shard_map/while/body/eval_jaxpr/add | solution.py:79
  895.4 7.0 collective-permute-start.12
  904.3 9.1 collective-permute-start.14
  917.9 7.1 collective-permute-done.15
  930.4 9.4 fusion.32
  959.3 9.1 collective-permute-done.19
  976.4 8.6 fusion.26
  (256 shorter events, 382.1 us)
Async XLA Ops:
  0.0 16.0 %copy-start.4 = (f32[5,16,16,256]{3,2,1,0:T(8,128)S(1)}, f32[5,16,16,256]{3,2,1,0:T(8,128)}, u32[]{:S(2)}) copy-start(f32[5,16,16,256]{3,2,1,0:T(8,128)} %param.10) | copy-start | bytes 3932164
  2.3 128.0 %collective-permute-start.6 = (bf16[16,5,1,16,256]{4,3,2,1,0:T(8,128)(2,1)}, bf16[16,5,1,16,256]{4,3,2,1,0:T(8,128)(2,1)}, u32[]{:S(2)}, u32[]{:S(2)}) collective-permute-start(bf16[16,5,1,16,256]{4,3,2,1,0:T(8,128)(2,1)} %get-tuple-element.204), channel_id=1, source_target_pairs={{0,32},{32,64},{64,96},{1,33},{33,65},{65,97},{2,34},{34,66},{66,9... | collective-permute-start | bytes 1966088 | tf_op jit(solution)/shard_map/ppermute | solution.py:21
  6.0 146.3 %collective-permute-start.7 = (bf16[16,5,1,16,256]{4,3,2,1,0:T(8,128)(2,1)S(1)}, bf16[16,5,1,16,256]{4,3,2,1,0:T(8,128)(2,1)}, u32[]{:S(2)}, u32[]{:S(2)}) collective-permute-start(bf16[16,5,1,16,256]{4,3,2,1,0:T(8,128)(2,1)S(1)} %get-tuple-element.203), channel_id=1, source_target_pairs={{32,0},{64,32},{96,64},{33,1},{65,33},{97,65},{34,2},{66,34},{98,6... | collective-permute-start | bytes 1966088 | tf_op jit(solution)/shard_map/ppermute | solution.py:23
  10.4 157.1 %collective-permute-start.2 = (bf16[16,5,1,16,256]{4,3,2,1,0:T(8,128)(2,1)}, bf16[16,5,1,16,256]{4,3,2,1,0:T(8,128)(2,1)}, u32[]{:S(2)}, u32[]{:S(2)}) collective-permute-start(bf16[16,5,1,16,256]{4,3,2,1,0:T(8,128)(2,1)} %get-tuple-element.206), channel_id=1, source_target_pairs={{0,32},{32,64},{64,96},{1,33},{33,65},{65,97},{2,34},{34,66},{66,9... | collective-permute-start | bytes 1966088 | tf_op jit(solution)/shard_map/ppermute | solution.py:21
  14.1 175.1 %collective-permute-start.3 = (bf16[16,5,1,16,256]{4,3,2,1,0:T(8,128)(2,1)}, bf16[16,5,1,16,256]{4,3,2,1,0:T(8,128)(2,1)}, u32[]{:S(2)}, u32[]{:S(2)}) collective-permute-start(bf16[16,5,1,16,256]{4,3,2,1,0:T(8,128)(2,1)} %get-tuple-element.205), channel_id=1, source_target_pairs={{32,0},{64,32},{96,64},{33,1},{65,33},{97,65},{34,2},{66,34},{98,6... | collective-permute-start | bytes 1966088 | tf_op jit(solution)/shard_map/ppermute | solution.py:23
  16.9 94.0 %copy-start.1 = (f32[5,16,16,256]{3,0,2,1:T(8,128)}, f32[5,16,16,256]{3,0,2,1:T(8,128)S(1)}, u32[]{:S(2)}) copy-start(f32[5,16,16,256]{3,0,2,1:T(8,128)S(1)} %copy.42) | copy-start | bytes 3932164
  17.6 95.0 %collective-permute-start.1 = (f32[5,1,16,256]{3,0,2,1:T(8,128)S(1)}, f32[5,1,16,256]{3,0,2,1:T(8,128)S(1)}, u32[]{:S(2)}, u32[]{:S(2)}) collective-permute-start(f32[5,1,16,256]{3,0,2,1:T(8,128)S(1)} %get-tuple-element.232), channel_id=1, source_target_pairs={{0,32},{32,64},{64,96},{1,33},{33,65},{65,97},{2,34},{34,66},{66,9... | collective-permute-start | bytes 245768 | tf_op jit(solution)/shard_map/ppermute | solution.py:21
  112.6 39.8 %copy-start.12 = (f32[5,1,16,256]{3,0,2,1:T(8,128)}, f32[5,1,16,256]{3,0,2,1:T(8,128)S(1)}, u32[]{:S(2)}) copy-start(f32[5,1,16,256]{3,0,2,1:T(8,128)S(1)} %collective-permute-done.1) | copy-start | bytes 245764
  112.6 778.4 %collective-permute-start = (f32[5,1,16,256]{3,0,2,1:T(8,128)}, f32[5,1,16,256]{3,0,2,1:T(8,128)}, u32[]{:S(2)}, u32[]{:S(2)}) collective-permute-start(f32[5,1,16,256]{3,0,2,1:T(8,128)} %get-tuple-element.231), channel_id=1, source_target_pairs={{32,0},{64,32},{96,64},{33,1},{65,33},{97,65},{34,2},{66,34},{98,6... | collective-permute-start | bytes 245768 | tf_op jit(solution)/shard_map/ppermute | solution.py:23
  156.0 47.8 %collective-permute-start.8 = (bf16[16,5,18,1,256]{4,0,3,2,1:T(8,128)(2,1)S(1)}, bf16[16,5,18,1,256]{4,0,3,2,1:T(8,128)(2,1)S(1)}, u32[]{:S(2)}, u32[]{:S(2)}) collective-permute-start(bf16[16,5,18,1,256]{4,0,3,2,1:T(8,128)(2,1)S(1)} %get-tuple-element.199), channel_id=1, source_target_pairs={{0,1},{1,2},{2,3},{3,4},{4,5},{5,6},{6,7},{7,8},{8,9},{9,10},{10,1... | collective-permute-start | bytes 2211848 | tf_op jit(solution)/shard_map/ppermute | solution.py:21
  165.6 38.2 %collective-permute-start.9 = (bf16[16,5,18,1,256]{4,0,3,2,1:T(8,128)(2,1)S(1)}, bf16[16,5,18,1,256]{4,0,3,2,1:T(8,128)(2,1)S(1)}, u32[]{:S(2)}, u32[]{:S(2)}) collective-permute-start(bf16[16,5,18,1,256]{4,0,3,2,1:T(8,128)(2,1)S(1)} %get-tuple-element.200), channel_id=1, source_target_pairs={{1,0},{2,1},{3,2},{4,3},{5,4},{6,5},{7,6},{8,7},{9,8},{10,9},{11,1... | collective-permute-start | bytes 2211848 | tf_op jit(solution)/shard_map/ppermute | solution.py:23
  192.8 32.4 %collective-permute-start.4 = (bf16[16,5,18,1,256]{4,0,3,2,1:T(8,128)(2,1)S(1)}, bf16[16,5,18,1,256]{4,0,3,2,1:T(8,128)(2,1)S(1)}, u32[]{:S(2)}, u32[]{:S(2)}) collective-permute-start(bf16[16,5,18,1,256]{4,0,3,2,1:T(8,128)(2,1)S(1)} %get-tuple-element.201), channel_id=1, source_target_pairs={{0,1},{1,2},{2,3},{3,4},{4,5},{5,6},{6,7},{7,8},{8,9},{9,10},{10,1... | collective-permute-start | bytes 2211848 | tf_op jit(solution)/shard_map/ppermute | solution.py:21
  201.9 25.5 %collective-permute-start.5 = (bf16[16,5,18,1,256]{4,0,3,2,1:T(8,128)(2,1)S(1)}, bf16[16,5,18,1,256]{4,0,3,2,1:T(8,128)(2,1)S(1)}, u32[]{:S(2)}, u32[]{:S(2)}) collective-permute-start(bf16[16,5,18,1,256]{4,0,3,2,1:T(8,128)(2,1)S(1)} %get-tuple-element.202), channel_id=1, source_target_pairs={{1,0},{2,1},{3,2},{4,3},{5,4},{6,5},{7,6},{8,7},{9,8},{10,9},{11,1... | collective-permute-start | bytes 2211848 | tf_op jit(solution)/shard_map/ppermute | solution.py:23
  203.8 23.5 %slice-start = ((s8[11796480]{0:T(1024)(128)(4,1)}), s8[4194304]{0:T(1024)(128)(4,1)S(1)}, s32[]{:S(2)}) async-start(s8[11796480]{0:T(1024)(128)(4,1)} %bitcast.119), calls=%async_computation | async-start | bytes 8388608
  203.8 23.5 %slice-start.1 = ((s8[11796480]{0:T(1024)(128)(4,1)}), s8[4194304]{0:T(1024)(128)(4,1)S(1)}, s32[]{:S(2)}) async-start(s8[11796480]{0:T(1024)(128)(4,1)} %bitcast.119), calls=%async_computation.1 | async-start | bytes 8388608
  211.6 15.7 %slice-start.2 = ((s8[11796480]{0:T(1024)(128)(4,1)}), s8[3407872]{0:T(1024)(128)(4,1)S(1)}, s32[]{:S(2)}) async-start(s8[11796480]{0:T(1024)(128)(4,1)} %bitcast.119), calls=%async_computation.2 | async-start | bytes 6815744
  229.1 13.5 %copy-start.17 = (s32[16]{0:T(128)S(1)}, s32[16]{0:T(128)}, u32[]{:S(2)}) copy-start(s32[16]{0:T(128)} %param.12) | copy-start | bytes 196
  242.7 630.4 %copy-start.14 = (f32[16,16,256]{2,1,0:T(8,128)S(1)}, f32[16,16,256]{2,1,0:T(8,128)}, u32[]{:S(2)}) copy-start(f32[16,16,256]{2,1,0:T(8,128)} %get-tuple-element.238) | copy-start | bytes 786436
  299.1 7.6 copy-start
  338.6 7.6 copy-start
  378.0 7.6 copy-start
  417.4 7.6 copy-start
  456.8 7.6 copy-start
  496.3 7.6 copy-start
  535.7 7.6 copy-start
  575.1 7.6 copy-start
  614.5 7.6 copy-start
  654.0 7.6 copy-start
  693.4 7.6 copy-start
  772.3 7.6 copy-start
  851.1 7.6 copy-start
  884.3 7.7 collective-permute-start.10
  889.1 6.3 collective-permute-start.11
  895.4 19.9 %collective-permute-start.12 = (f32[5,18,1,256]{3,0,2,1:T(8,128)S(1)}, f32[5,18,1,256]{3,0,2,1:T(8,128)S(1)}, u32[]{:S(2)}, u32[]{:S(2)}) collective-permute-start(f32[5,18,1,256]{3,0,2,1:T(8,128)S(1)} %get-tuple-element.215), channel_id=1, source_target_pairs={{0,1},{1,2},{2,3},{3,4},{4,5},{5,6},{6,7},{7,8},{8,9},{9,10},{10,1... | collective-permute-start | bytes 276488 | tf_op jit(solution)/shard_map/ppermute | solution.py:21
  902.4 13.0 %collective-permute-start.13 = (f32[5,18,1,256]{3,0,2,1:T(8,128)S(1)}, f32[5,18,1,256]{3,0,2,1:T(8,128)S(1)}, u32[]{:S(2)}, u32[]{:S(2)}) collective-permute-start(f32[5,18,1,256]{3,0,2,1:T(8,128)S(1)} %get-tuple-element.216), channel_id=1, source_target_pairs={{1,0},{2,1},{3,2},{4,3},{5,4},{6,5},{7,6},{8,7},{9,8},{10,9},{11,1... | collective-permute-start | bytes 276488 | tf_op jit(solution)/shard_map/ppermute | solution.py:23
  904.3 13.6 %collective-permute-start.14 = (f32[5,18,1,256]{3,0,2,1:T(8,128)S(1)}, f32[5,18,1,256]{3,0,2,1:T(8,128)S(1)}, u32[]{:S(2)}, u32[]{:S(2)}) collective-permute-start(f32[5,18,1,256]{3,0,2,1:T(8,128)S(1)} %get-tuple-element.213), channel_id=1, source_target_pairs={{0,1},{1,2},{2,3},{3,4},{4,5},{5,6},{6,7},{7,8},{8,9},{9,10},{10,1... | collective-permute-start | bytes 276488 | tf_op jit(solution)/shard_map/ppermute | solution.py:21
  913.4 11.6 %collective-permute-start.15 = (f32[5,18,1,256]{3,0,2,1:T(8,128)S(1)}, f32[5,18,1,256]{3,0,2,1:T(8,128)S(1)}, u32[]{:S(2)}, u32[]{:S(2)}) collective-permute-start(f32[5,18,1,256]{3,0,2,1:T(8,128)S(1)} %get-tuple-element.214), channel_id=1, source_target_pairs={{1,0},{2,1},{3,2},{4,3},{5,4},{6,5},{7,6},{8,7},{9,8},{10,9},{11,1... | collective-permute-start | bytes 276488 | tf_op jit(solution)/shard_map/ppermute | solution.py:23
  917.9 12.5 %copy-start.10 = (f32[5,18,18,256]{3,0,2,1:T(8,128)}, f32[5,18,18,256]{3,0,2,1:T(8,128)S(1)}, u32[]{:S(2)}) copy-start(f32[5,18,18,256]{3,0,2,1:T(8,128)S(1)} %convolution_bitcast_fusion.4) | copy-start | bytes 4976644
  917.9 12.5 %copy-start.2 = (f32[5,16,16,256]{3,0,2,1:T(8,128)S(1)}, f32[5,16,16,256]{3,0,2,1:T(8,128)}, u32[]{:S(2)}) copy-start(f32[5,16,16,256]{3,0,2,1:T(8,128)} %copy-done.1) | copy-start | bytes 3932164
  917.9 12.5 %copy-start.6 = (f32[5,16,16,255]{3,0,2,1:T(8,128)S(1)}, f32[5,16,16,255]{3,0,2,1:T(8,128)}, u32[]{:S(2)}) copy-start(f32[5,16,16,255]{3,0,2,1:T(8,128)} %get-tuple-element.223) | copy-start | bytes 3916804
  917.9 12.5 %copy-start.7 = (f32[5,16,16,255]{3,0,2,1:T(8,128)S(1)}, f32[5,16,16,255]{3,0,2,1:T(8,128)}, u32[]{:S(2)}) copy-start(f32[5,16,16,255]{3,0,2,1:T(8,128)} %get-tuple-element.224) | copy-start | bytes 3916804
  917.9 12.5 %copy-start.8 = (f32[5,16,16,1]{3,0,2,1:T(8,128)S(1)}, f32[5,16,16,1]{3,0,2,1:T(8,128)}, u32[]{:S(2)}) copy-start(f32[5,16,16,1]{3,0,2,1:T(8,128)} %get-tuple-element.225) | copy-start | bytes 15364
  917.9 12.5 %copy-start.9 = (f32[5,16,16,1]{3,0,2,1:T(8,128)S(1)}, f32[5,16,16,1]{3,0,2,1:T(8,128)}, u32[]{:S(2)}) copy-start(f32[5,16,16,1]{3,0,2,1:T(8,128)} %get-tuple-element.226) | copy-start | bytes 15364
  917.9 12.5 %copy-start.13 = (f32[5,1,16,256]{3,0,2,1:T(8,128)S(1)}, f32[5,1,16,256]{3,0,2,1:T(8,128)}, u32[]{:S(2)}) copy-start(f32[5,1,16,256]{3,0,2,1:T(8,128)} %copy-done.12) | copy-start | bytes 245764
  943.9 7.8 collective-permute-start.16
  947.1 6.3 collective-permute-start.17
  953.4 5.9 collective-permute-start.18
  956.8 11.6 %collective-permute-start.19 = (f32[5,18,1,256]{3,0,2,1:T(8,128)S(1)}, f32[5,18,1,256]{3,0,2,1:T(8,128)S(1)}, u32[]{:S(2)}, u32[]{:S(2)}) collective-permute-start(f32[5,18,1,256]{3,0,2,1:T(8,128)S(1)} %get-tuple-element.212), channel_id=1, source_target_pairs={{1,0},{2,1},{3,2},{4,3},{5,4},{6,5},{7,6},{8,7},{9,8},{10,9},{11,1... | collective-permute-start | bytes 276488 | tf_op jit(solution)/shard_map/ppermute | solution.py:23
  (8 other events, 37.7 us)
